TPU v7x, 32 devices: a whole 2x2x4 slice. The times are simulated.
32 devices in a mesh: grp: 4 (over y, x), tile: 8 (over z, core).
Axes of the slice: x: 2, y: 2, z: 4, core: 2. Of those that a mesh axis runs over, the one named last changes fastest.
Arguments:
- flow_fields: float32 [5, 256, 16, 128], P(None, 'tile', 'grp'), may hold values from -6 to 6
- turbulent_diffusivity: float32 [256, 16, 128], P('tile', 'grp'), may hold values from 0.05 to 0.3
- holder_unit: int32 [4, 256, 1], P('grp', 'tile'), may hold values from 0 to 7, as said below
- spray_volume_position: int32 [8, 1024, 128], P('tile'), may hold values from 0 to 511
- patch_pick_unreduced: int32 [8, 1024], P('tile'), may hold values from 0 to 1048575
- droplet_motion: float32 [8, 1024, 3, 128], P('tile'), may hold values from -6 to 6
- droplet_warmth: float32 [8, 1024, 128], P('tile'), may hold values from -6 to 6
- droplet_weightiness: float32 [8, 1024, 128], P('tile'), may hold values from 0.25 to 2
- droplet_multiplicity: float32 [8, 1024, 128], P('tile'), may hold values from 0.5 to 2
- living_spray_batches: int32 [8], P('tile'), may hold values from 1 to 1024, 4096 in all
Outputs:
- gas_next: float32 [5, 256, 16, 128], P(None, 'tile', 'grp')
Inputs may be any that keep to these rules, and one draw needn't show every extreme that they name: `holder_unit`: among the 32 tiles of one gas device (aligned blocks of 32 rows of owner, in order of its first two dimensions) no parcel device owns more than 8, and in every such block one parcel device owns exactly 8. Two parcel devices own no tile at all. Rows with g = 3 are not used. `living_spray_batches`: live blocks of a device are its first ones; the busiest parcel device has exactly 1024, and they sum to 4096.
All inputs are finite; a program needn't handle non-finite values.
Results may differ from a plain program's by a relative error of at most 0.0045.
Values may be sent and summed in bfloat16 or wider, within the bound.
A program may use at most 64 MiB of HBM per device.

v0:
```python
import jax
import jax.numpy as jnp
from jax import lax
from jax.sharding import PartitionSpec as P

BLOCK_GROUP = 64


def padded_2(block, sides, width):
    for axis, dim in sides:
        count = lax.axis_size(axis)
        forward = [(i, i + 1) for i in range(count - 1)]
        backward = [(target, source) for source, target in forward]
        low = lax.ppermute(
            lax.slice_in_dim(block, block.shape[dim] - width, None, axis=dim), axis, forward
        )
        high = lax.ppermute(lax.slice_in_dim(block, 0, width, axis=dim), axis, backward)
        block = jnp.concatenate([low, block, high], axis=dim)
    return block


def droplet_coupling_feeds(
    reached_markers, droplet_motion, droplet_warmth, droplet_weightiness, droplet_multiplicity
):
    gas_velocity = reached_markers[..., 0:3, :]
    fluid_warming_share = reached_markers[..., 3, :]
    gas_fuel = reached_markers[..., 4, :]
    relative = gas_velocity - droplet_motion
    speed_sq = jnp.sum(relative * relative, axis=-2)
    surface = droplet_weightiness ** (2.0 / 3.0)
    inverse_tau = 0.8 * (1.0 + 0.15 * (1.0 + speed_sq) ** 0.3435) / surface
    relaxation = 1.0 - jnp.exp(-0.5 * inverse_tau)
    new_velocity = droplet_motion + relaxation[..., None, :] * relative
    heating = 1.0 / (1.0 + jnp.exp(-(fluid_warming_share - gas_fuel)))
    leftover_liquid_load = jnp.exp(-0.3 * heating / surface)
    updated_droplet_load = droplet_weightiness * leftover_liquid_load
    warming_speed = 1.0 - jnp.exp(-0.25 * inverse_tau)
    updated_droplet_warmth = (
        droplet_warmth
        + warming_speed * (fluid_warming_share - droplet_warmth)
        - 0.5 * (1.0 - leftover_liquid_load)
    )
    momentum = (
        droplet_weightiness[..., None, :] * droplet_motion
        - updated_droplet_load[..., None, :] * new_velocity
    )
    enthalpy_content = (
        droplet_weightiness * droplet_warmth - updated_droplet_load * updated_droplet_warmth
    )
    stacked = jnp.concatenate(
        [
            momentum,
            enthalpy_content[..., None, :],
            (droplet_weightiness - updated_droplet_load)[..., None, :],
        ],
        axis=-2,
    )
    return droplet_multiplicity[..., None, :] * stacked


def local(
    flow_fields,
    turbulent_diffusivity,
    holder_unit,
    spray_volume_position,
    patch_pick_unreduced,
    droplet_motion,
    droplet_warmth,
    droplet_weightiness,
    droplet_multiplicity,
    living_spray_batches,
):
    group_count = lax.axis_size("grp")
    owners = lax.axis_size("tile")
    group_index = lax.axis_index("grp")
    gas_side = (group_index < group_count - 1).astype(jnp.float32)
    gas_field = flow_fields * gas_side
    nfield, planes, rows_y, z_cells = gas_field.shape
    tile_cells = rows_y * z_cells
    slot_depth = max(2, 2 * planes // owners)
    padded = padded_2(gas_field.astype(jnp.bfloat16), (("grp", 2), ("tile", 1)), 1).astype(
        gas_field.dtype
    )
    z_padded = jnp.pad(gas_field, ((0, 0), (0, 0), (0, 0), (1, 1)))
    beside = padded[:, 2:, 1:-1, :] + padded[:, :-2, 1:-1, :]
    beside = beside + padded[:, 1:-1, 2:, :] + padded[:, 1:-1, :-2, :]
    beside = beside + z_padded[:, :, :, 2:] + z_padded[:, :, :, :-2]
    laplace = beside - 6.0 * gas_field
    plane_owner = holder_unit[0, :, 0]
    positions = jnp.arange(planes, dtype=jnp.int32)
    same_owner = plane_owner[:, None] == plane_owner[None, :]
    plane_rank = jnp.sum(
        (same_owner & (positions[None, :] < positions[:, None])).astype(jnp.int32), axis=1
    )
    targets = jnp.arange(owners * slot_depth, dtype=jnp.int32)
    selector = (
        (plane_owner[None, :] == targets[:, None] // slot_depth)
        & (plane_rank[None, :] == targets[:, None] % slot_depth)
    ).astype(jnp.float32) * gas_side
    tile_rows = (
        gas_field.astype(jnp.bfloat16).transpose(1, 0, 2, 3).reshape(planes, nfield * tile_cells)
    )
    packed = jnp.dot(selector.astype(jnp.bfloat16), tile_rows, preferred_element_type=jnp.float32)
    packed = packed.astype(jnp.bfloat16).reshape(owners, slot_depth, nfield, tile_cells)
    slot_flags = jnp.sum(selector, axis=1).astype(jnp.int32).reshape(owners, slot_depth)
    lifted_tiles, lifted_flags = (
        lax.all_gather(packed[None], "grp", axis=0, tiled=True),
        lax.all_gather(slot_flags[None], "grp", axis=0, tiled=True),
    )
    arrived, arrived_flags = (
        lax.all_to_all(lifted_tiles, "tile", split_axis=1, concat_axis=1, tiled=True),
        lax.all_to_all(lifted_flags, "tile", split_axis=1, concat_axis=1, tiled=True),
    )
    gas_groups = group_count - 1
    slot_count = gas_groups * owners * slot_depth
    tile_table = arrived[:gas_groups].reshape(slot_count, nfield, tile_cells)
    valid = arrived_flags[:gas_groups].reshape(slot_count)
    owned_count = jnp.sum(valid)
    running = jnp.cumsum(valid)
    picked = patch_pick_unreduced[0] % jnp.maximum(owned_count, 1)
    matches = (valid[None, :] == 1) & (running[None, :] - 1 == picked[:, None])
    block_slot = jnp.sum(
        jnp.where(matches, jnp.arange(slot_count, dtype=jnp.int32)[None, :], 0), axis=1
    )
    live_count = living_spray_batches[0]
    share_size = (
        (live_count + group_count * BLOCK_GROUP - 1) // (group_count * BLOCK_GROUP) * BLOCK_GROUP
    )
    first_block = jnp.minimum(group_index * share_size, live_count)
    end_block = jnp.minimum(first_block + share_size, live_count)
    end_block = jnp.where(owned_count > 0, end_block, first_block)
    group_turns = (end_block - first_block + BLOCK_GROUP - 1) // BLOCK_GROUP
    parcel_cells = spray_volume_position[0]
    parcel_velocity = droplet_motion[0]
    droplet_warming_share = droplet_warmth[0]
    parcel_mass = droplet_weightiness[0]
    parcel_weight = droplet_multiplicity[0]
    cell_ids = jnp.arange(tile_cells, dtype=jnp.int32)

    def advance(step_index, totals):
        start = first_block + step_index * BLOCK_GROUP

        def block_slice(array):
            return lax.dynamic_slice_in_dim(array, start, BLOCK_GROUP, 0)

        block_ids = start + jnp.arange(BLOCK_GROUP, dtype=jnp.int32)
        keep_mask = (block_ids < end_block).astype(jnp.float32)
        slots_here = block_slice(block_slot)
        cells_here = block_slice(parcel_cells)
        tile_values = tile_table[slots_here]
        one_hot = (cells_here[:, :, None] == cell_ids[None, None, :]).astype(jnp.bfloat16)
        reached_markers = jnp.einsum(
            "bfc,bpc->bfp", tile_values, one_hot, preferred_element_type=jnp.float32
        )
        coupling_feeds = droplet_coupling_feeds(
            reached_markers,
            block_slice(parcel_velocity),
            block_slice(droplet_warming_share),
            block_slice(parcel_mass),
            block_slice(parcel_weight),
        )
        coupling_feeds = coupling_feeds * keep_mask[:, None, None]
        upper = coupling_feeds.astype(jnp.bfloat16)
        leftover = coupling_feeds - upper.astype(jnp.float32)
        middle = leftover.astype(jnp.bfloat16)
        lower = (leftover - middle.astype(jnp.float32)).astype(jnp.bfloat16)
        pieces = jnp.concatenate([upper, middle, lower], axis=1)
        deposited = jnp.einsum("bfp,bpc->bfc", pieces, one_hot, preferred_element_type=jnp.float32)
        per_block = (
            deposited[:, :nfield] + deposited[:, nfield : 2 * nfield] + deposited[:, 2 * nfield :]
        )
        return totals.at[slots_here].add(per_block)

    deposit = lax.fori_loop(
        0, group_turns, advance, jnp.zeros((slot_count, nfield, tile_cells), jnp.float32)
    )
    zero_block = jnp.zeros((1, owners, slot_depth, nfield, tile_cells), jnp.float32)
    outgoing = jnp.concatenate(
        [deposit.reshape(gas_groups, owners, slot_depth, nfield, tile_cells), zero_block], axis=0
    )
    spread = lax.all_to_all(outgoing, "tile", split_axis=1, concat_axis=1, tiled=True)
    landed = lax.psum_scatter(spread, "grp", scatter_dimension=0, tiled=True)
    incoming = landed.reshape(owners * slot_depth, nfield * tile_cells)
    placed = jnp.dot(
        selector.T, incoming, precision=lax.Precision.HIGHEST, preferred_element_type=jnp.float32
    )
    placed = placed.reshape(planes, nfield, rows_y, z_cells).transpose(1, 0, 2, 3)
    return (gas_field + 0.5 * turbulent_diffusivity * laplace + placed) * gas_side


def solution(mesh):
    in_specs = (
        P(None, "tile", "grp", None),
        P("tile", "grp", None),
        P("grp", "tile", None),
        P("tile", None, None),
        P("tile", None),
        P("tile", None, None, None),
        P("tile", None, None),
        P("tile", None, None),
        P("tile", None, None),
        P("tile"),
    )
    out_specs = P(None, "tile", "grp", None)
    return jax.shard_map(local, mesh=mesh, in_specs=in_specs, out_specs=out_specs, check_vma=False)
```

profile of v0, /device:TPU:0, one launch (start us, length us, event | category | flops | bytes accessed | tf_op | source)
XLA Modules:
  0.0 326.9 jit_solution(9831295287302092745)
XLA Ops:
  6.5 0.9 convert_reduce_fusion
  7.5 1.0 fusion.40
  8.7 1.7 convolution_convert_fusion
  10.4 0.7 select_reduce_fusion.1
  11.2 9.7 %all_gather.6 = s32[4,8,8]{2,1,0:T(8,128)S(1)} all-gather(s32[1,8,8]{2,1,0:T(8,128)S(1)} %convert_element_type.87), channel_id=1, replica_groups=mesh['grp'=4,'tile'=8] {'grp'}, dimensions={0}, use_global_device_ids=true | all-gather | bytes 1280 | tf_op jit(solution)/shard_map/all_gather | solution.py:108
  20.9 0.6 copy.79
  21.5 4.9 %all-to-all-start = ((s32[4,8,8]{2,0,1:T(4,128)}), s32[4,8,8]{2,0,1:T(4,128)S(1)}, u32[]{:S(2)}, u32[]{:S(2)}) async-start(s32[4,8,8]{2,0,1:T(4,128)} %copy.79), calls=%async_computation | async-start | bytes 32768 | tf_op jit(solution)/shard_map/all_to_all | solution.py:112
  26.4 15.6 %all-gather.2.cloned.1.call-done = bf16[4,8,8,5,512]{4,2,3,1,0:T(8,128)(2,1)} async-done(((bf16[1,8,8,5,512]{4,2,3,1,0:T(8,128)(2,1)}), bf16[4,8,8,5,512]{4,2,3,1,0:T(8,128)(2,1)}) %all-gather.2.cloned.1.call-update) | async-done | bytes 1310736 | tf_op jit(solution)/shard_map/all_gather | solution.py:107
  41.9 2.5 copy.83
  44.5 4.7 %all-to-all-start.1 = ((bf16[4,8,8,5,512]{4,2,3,0,1:T(8,128)(2,1)}), bf16[4,8,8,5,512]{4,2,3,0,1:T(8,128)(2,1)S(1)}, u32[]{:S(2)}, u32[]{:S(2)}) async-start(bf16[4,8,8,5,512]{4,2,3,0,1:T(8,128)(2,1)} %copy.83), calls=%async_computation.1 | async-start | bytes 2621440 | tf_op jit(solution)/shard_map/all_to_all | solution.py:111
  49.9 2.5 copy.105
  52.4 0.7 fusion.43
  55.7 25.7 %all-to-all-done.1 = bf16[4,8,8,5,512]{4,2,3,0,1:T(8,128)(2,1)S(1)} async-done(((bf16[4,8,8,5,512]{4,2,3,0,1:T(8,128)(2,1)}), bf16[4,8,8,5,512]{4,2,3,0,1:T(8,128)(2,1)S(1)}, u32[]{:S(2)}, u32[]{:S(2)}) %all-to-all-start.1) | async-done | bytes 1310752 | tf_op jit(solution)/shard_map/all_to_all | solution.py:111
  81.6 0.6 copy.85
  82.2 2.1 broadcast_in_dim.54
  84.2 44.5 %while.14 = (s32[]{:T(128)}, f32[192,5,512]{2,1,0:T(8,128)}, s32[]{:T(128)}, s32[]{:T(128)}, s32[1024]{0:T(1024)S(1)}, /*index=5*/f32[1024,128]{1,0:T(8,128)}, f...) while((s32[]{:T(128)}, f32[192,5,512]{2,1,0:T(8,128)}, ...), condition=%wide.region_9.10_spmd.clone, body=%wide.region_6.9_spmd.clone.sunk | while | flops 178324864 | bytes 9770991 | solution.py:174
  84.3 0.6 gather_fusion
  84.9 0.8 constant_dynamic-slice_fusion.6
  85.7 4.3 %fusion.55 = f32[64,5,128]{2,1,0:T(8,128)S(1)} fusion(bf16[64,5,512]{2,1,0:T(8,128)(2,1)S(1)} %gather_fusion, s32[64,128]{1,0:T(8,128)S(1)} %constant_dynamic-slice_fusion.6), kind=kOutput, calls=%fused_computation.5.clone.1 | convolution fusion | flops 46137344 | bytes 524288 | tf_op jit(solution)/shard_map/while/body/bfc,bpc->bfp/dot_general | solution.py:152
  90.1 0.8 fusion.57
  91.0 1.0 multiply_reduce_fusion.2
  92.0 0.9 multiply_subtract_fusion.4
  92.9 1.0 multiply_subtract_fusion.5
  94.1 4.1 %fusion.59 = f32[64,15,512]{2,1,0:T(8,128)S(1)} fusion(s32[64,128]{1,0:T(8,128)S(1)} %constant_dynamic-slice_fusion.6, bf16[64,5,128]{2,1,0:T(8,128)(2,1)S(1)} %get-tuple-element.392, bf16[64,5,128]{2,1,0:T(8,128)(2,1)S(1)} %get-tuple-element.393, bf16[64,5,128]{2,1,0:T(8,128)(2,1)S(1)} %get-tuple-element.394), kind=kOutput, calls=%fused_computation.4.clone.1 | convolution fusion | flops 130760704 | bytes 2244608 | tf_op jit(solution)/shard_map/while/body/bfp,bpc->bfc/dot_general | solution.py:168
  98.4 8.1 %scatter_fusion = f32[192,5,512]{2,1,0:T(8,128)} fusion(f32[192,5,512]{2,1,0:T(8,128)} %get-tuple-element.412, s32[64]{0:T(128)S(1)} %compare_select_fusion.2, f32[64,5,512]{2,1,0:T(8,128)S(1)} %slice_add_fusion.7), kind=kCustom, calls=%fused_computation.1.clone.clone.1 | custom fusion | flops 163840 | bytes 1966336 | tf_op jit(solution)/shard_map/while/body/scatter-add | solution.py:172
  106.5 0.6 gather_fusion
  107.1 0.8 constant_dynamic-slice_fusion.6
  107.9 4.3 %fusion.55 = f32[64,5,128]{2,1,0:T(8,128)S(1)} fusion(bf16[64,5,512]{2,1,0:T(8,128)(2,1)S(1)} %gather_fusion, s32[64,128]{1,0:T(8,128)S(1)} %constant_dynamic-slice_fusion.6), kind=kOutput, calls=%fused_computation.5.clone.1 | convolution fusion | flops 46137344 | bytes 524288 | tf_op jit(solution)/shard_map/while/body/bfc,bpc->bfp/dot_general | solution.py:152
  112.3 0.8 fusion.57
  113.2 1.0 multiply_reduce_fusion.2
  114.2 0.9 multiply_subtract_fusion.4
  115.1 1.0 multiply_subtract_fusion.5
  116.3 4.1 %fusion.59 = f32[64,15,512]{2,1,0:T(8,128)S(1)} fusion(s32[64,128]{1,0:T(8,128)S(1)} %constant_dynamic-slice_fusion.6, bf16[64,5,128]{2,1,0:T(8,128)(2,1)S(1)} %get-tuple-element.392, bf16[64,5,128]{2,1,0:T(8,128)(2,1)S(1)} %get-tuple-element.393, bf16[64,5,128]{2,1,0:T(8,128)(2,1)S(1)} %get-tuple-element.394), kind=kOutput, calls=%fused_computation.4.clone.1 | convolution fusion | flops 130760704 | bytes 2244608 | tf_op jit(solution)/shard_map/while/body/bfp,bpc->bfc/dot_general | solution.py:168
  120.6 8.1 %scatter_fusion = f32[192,5,512]{2,1,0:T(8,128)} fusion(f32[192,5,512]{2,1,0:T(8,128)} %get-tuple-element.412, s32[64]{0:T(128)S(1)} %compare_select_fusion.2, f32[64,5,512]{2,1,0:T(8,128)S(1)} %slice_add_fusion.7), kind=kCustom, calls=%fused_computation.1.clone.clone.1 | custom fusion | flops 163840 | bytes 1966336 | tf_op jit(solution)/shard_map/while/body/scatter-add | solution.py:172
  128.7 3.0 copy.98
  132.1 105.3 %all_to_all.15 = f32[4,8,8,5,512]{4,2,0,3,1:T(8,128)S(1)} all-to-all(f32[4,8,8,5,512]{4,2,0,3,1:T(8,128)S(1)} %concatenate.25.clone), channel_id=1, replica_groups=mesh['grp'=4,'tile'=8] {'tile'}, dimensions={1} | all-to-all | bytes 5242880 | tf_op jit(solution)/shard_map/all_to_all | solution.py:181
  237.4 1.8 copy.88
  239.2 3.4 %collective-permute-start = (bf16[5,32,1,128]{3,1,2,0:T(8,128)(2,1)S(1)}, bf16[5,32,1,128]{3,1,2,0:T(8,128)(2,1)S(1)}, u32[]{:S(2)}, u32[]{:S(2)}) collective-permute-start(bf16[5,32,1,128]{3,1,2,0:T(8,128)(2,1)S(1)} %get-tuple-element.293), channel_id=1, source_target_pairs={{0,8},{8,16},{16,24},{1,9},{9,17},{17,25},{2,10},{10,18},{18,26},{... | collective-permute-start | bytes 122888 | tf_op jit(solution)/shard_map/ppermute | solution.py:14
  242.7 1.3 collective-permute-start.1
  244.0 1.0 collective-permute-done
  245.0 4.6 %collective-permute-done.1 = bf16[5,32,1,128]{3,1,2,0:T(8,128)(2,1)S(1)} collective-permute-done((bf16[5,32,1,128]{3,1,2,0:T(8,128)(2,1)S(1)}, bf16[5,32,1,128]{3,1,2,0:T(8,128)(2,1)S(1)}, u32[]{:S(2)}, u32[]{:S(2)}) %collective-permute-start.1) | collective-permute-done | bytes 40992 | tf_op jit(solution)/shard_map/ppermute | solution.py:17
  249.6 1.3 collective-permute-start.2
  250.9 1.3 collective-permute-start.3
  252.9 1.1 collective-permute-done.3
  254.1 62.3 %all-reduce.6.cloned.1.call-done = f32[4,8,8,5,512]{4,2,1,0,3:T(8,128)} async-done(((f32[4,8,8,5,512]{4,2,1,0,3:T(8,128)}), f32[4,8,8,5,512]{4,2,1,0,3:T(8,128)}) %all-reduce.6.cloned.1.call-update) | async-done | bytes 2621456
  316.5 1.8 constant_dynamic-slice_fusion.3
  318.6 0.6 fusion.18
  319.2 0.9 copy.91
  (57 shorter events, 4.3 us)
Async XLA Ops:
  6.5 35.4 %all-gather.2.cloned.1.call-start = ((), (), s32[]{:S(2)}) async-start(), calls=%async_computation.3 | async-start | bytes 1638400 | tf_op jit(solution)/shard_map/all_gather | solution.py:107
  21.5 23.0 %all-to-all-start = ((s32[4,8,8]{2,0,1:T(4,128)}), s32[4,8,8]{2,0,1:T(4,128)S(1)}, u32[]{:S(2)}, u32[]{:S(2)}) async-start(s32[4,8,8]{2,0,1:T(4,128)} %copy.79), calls=%async_computation | async-start | bytes 32768 | tf_op jit(solution)/shard_map/all_to_all | solution.py:112
  26.4 23.5 %copy-start = (f32[1,1024,3,128]{3,1,2,0:T(8,128)S(1)}, f32[1,1024,3,128]{3,1,2,0:T(8,128)}, u32[]{:S(2)}) copy-start(f32[1,1024,3,128]{3,1,2,0:T(8,128)} %param.17) | copy-start | bytes 4718596
  44.5 10.6 %copy-start.2 = (s32[1,1024]{1,0:T(1,128)S(1)}, s32[1,1024]{1,0:T(1,128)}, u32[]{:S(2)}) copy-start(s32[1,1024]{1,0:T(1,128)} %param.16) | copy-start | bytes 12292
  44.5 36.9 %all-to-all-start.1 = ((bf16[4,8,8,5,512]{4,2,3,0,1:T(8,128)(2,1)}), bf16[4,8,8,5,512]{4,2,3,0,1:T(8,128)(2,1)S(1)}, u32[]{:S(2)}, u32[]{:S(2)}) async-start(bf16[4,8,8,5,512]{4,2,3,0,1:T(8,128)(2,1)} %copy.83), calls=%async_computation.1 | async-start | bytes 2621440 | tf_op jit(solution)/shard_map/all_to_all | solution.py:111
  49.2 267.3 %all-reduce.6.cloned.1.call-start = ((), (), s32[]{:S(2)}) async-start(), calls=%async_computation.4 | async-start | bytes 5242880
  239.2 13.0 %copy-start.1 = (f32[32,4,128]{2,1,0:T(4,128)S(1)}, f32[32,4,128]{2,1,0:T(4,128)}, u32[]{:S(2)}) copy-start(f32[32,4,128]{2,1,0:T(4,128)} %param.13) | copy-start | bytes 196612
  239.2 13.1 %copy-start.4 = (u32[32]{0:T(128)S(1)}, u32[32]{0:T(128)}, u32[]{:S(2)}) copy-start(u32[32]{0:T(128)} %constant.197) | copy-start | bytes 388
  239.2 5.7 %collective-permute-start = (bf16[5,32,1,128]{3,1,2,0:T(8,128)(2,1)S(1)}, bf16[5,32,1,128]{3,1,2,0:T(8,128)(2,1)S(1)}, u32[]{:S(2)}, u32[]{:S(2)}) collective-permute-start(bf16[5,32,1,128]{3,1,2,0:T(8,128)(2,1)S(1)} %get-tuple-element.293), channel_id=1, source_target_pairs={{0,8},{8,16},{16,24},{1,9},{9,17},{17,25},{2,10},{10,18},{18,26},{... | collective-permute-start | bytes 122888 | tf_op jit(solution)/shard_map/ppermute | solution.py:14
  242.7 6.9 %collective-permute-start.1 = (bf16[5,32,1,128]{3,1,2,0:T(8,128)(2,1)S(1)}, bf16[5,32,1,128]{3,1,2,0:T(8,128)(2,1)S(1)}, u32[]{:S(2)}, u32[]{:S(2)}) collective-permute-start(bf16[5,32,1,128]{3,1,2,0:T(8,128)(2,1)S(1)} %get-tuple-element.294), channel_id=1, source_target_pairs={{8,0},{16,8},{24,16},{9,1},{17,9},{25,17},{10,2},{18,10},{26,18},{... | collective-permute-start | bytes 122888 | tf_op jit(solution)/shard_map/ppermute | solution.py:17
  249.6 69.0 %copy-start.3 = (s32[1,32,1]{1,2,0:T(1,128)S(1)}, s32[1,32,1]{1,2,0:T(1,128)}, u32[]{:S(2)}) copy-start(s32[1,32,1]{1,2,0:T(1,128)} %param.14) | copy-start | bytes 388
  249.6 3.3 collective-permute-start.2
  250.9 3.1 collective-permute-start.3
Sparse Core Ops, SparseCore 0:
  10.5 31.3 all-gather.1
  239.3 77.0 all-reduce.5
where the time goes:
time: 330 us; the launch traced here: 327 us
  blocking collectives  115 us (35%)
  waiting for transfers between devices  110 us (33%)
  other arithmetic  29.2 us (9%)
  local copies, waits for them, and re-layouts  20.6 us (6%)
  matrix products  19.2 us (6%)
  starting transfers between devices  17 us (5%)
  between operations  15.6 us (5%)
    all_to_all x1, blocking collectives, local(): lax.all_to_all(outgoing, 'tile', split_axis=1, concat_axis=1, tiled=True)  105 us
    unnamed x3, waiting for transfers between devices  62.4 us
    all_to_all x1, waiting for transfers between devices, local(): lax.all_to_all(lifted_tiles, 'tile', split_axis=1, concat_axis=1, tiled=T...  25.7 us
    scatter-add x2, other arithmetic, advance(): return totals.at[slots_here].add(per_block)  16.1 us
    all_gather x1, waiting for transfers between devices, local(): lax.all_gather(packed[None], 'grp', axis=0, tiled=True)  15.6 us
    all_gather x1, blocking collectives, local(): lax.all_gather(slot_flags[None], 'grp', axis=0, tiled=True)  9.65 us
    dot_general x2, matrix products, advance(): jnp.einsum('bfc,bpc->bfp', tile_values, one_hot, preferred_element_type=j...  8.68 us
    unnamed x16, local copies, waits for them, and re-layouts  8.53 us
  transfers between devices with their start and end apart: 8, of which 6 were waited for; matrix products, arithmetic and copies ran while one was open for 3% of the time, Pallas kernels for 0%

commit v1 on v0

--- a/solution.py
+++ b/solution.py
@@ -178,7 +178,10 @@
     outgoing = jnp.concatenate(
         [deposit.reshape(gas_groups, owners, slot_depth, nfield, tile_cells), zero_block], axis=0
     )
-    spread = lax.all_to_all(outgoing, "tile", split_axis=1, concat_axis=1, tiled=True)
+    spread = jnp.concatenate(
+        lax.all_to_all(jnp.stack(jnp.split(outgoing, lax.axis_size("tile"), axis=1)), "tile", 0, 0),
+        axis=1,
+    )
     landed = lax.psum_scatter(spread, "grp", scatter_dimension=0, tiled=True)
     incoming = landed.reshape(owners * slot_depth, nfield * tile_cells)
     placed = jnp.dot(

time: 330 us -> 328 us (level)
    unnamed x16 -> x22, local copies, waits for them, and re-layouts: 8.53 us -> 5.68 us
where the time goes in v1:
time: 328 us; the launch traced here: 325 us
  blocking collectives  115 us (35%)
  waiting for transfers between devices  110 us (34%)
  other arithmetic  29.2 us (9%)
  matrix products  19.2 us (6%)
  local copies, waits for them, and re-layouts  18.6 us (6%)
  starting transfers between devices  17 us (5%)
  between operations  15.7 us (5%)
    all_to_all x1, blocking collectives, local(): lax.all_to_all(jnp.stack(jnp.split(outgoing, lax.axis_size('tile'), axis=...  105 us
    unnamed x3, waiting for transfers between devices  62.4 us
    all_to_all x1, waiting for transfers between devices, local(): lax.all_to_all(lifted_tiles, 'tile', split_axis=1, concat_axis=1, tiled=T...  25.7 us
    scatter-add x2, other arithmetic, advance(): return totals.at[slots_here].add(per_block)  16.1 us
    all_gather x1, waiting for transfers between devices, local(): lax.all_gather(packed[None], 'grp', axis=0, tiled=True)  15.6 us
    all_gather x1, blocking collectives, local(): lax.all_gather(slot_flags[None], 'grp', axis=0, tiled=True)  9.65 us
    dot_general x2, matrix products, advance(): jnp.einsum('bfc,bpc->bfp', tile_values, one_hot, preferred_element_type=j...  8.68 us
    dot_general x2, matrix products, advance(): jnp.einsum('bfp,bpc->bfc', pieces, one_hot, preferred_element_type=jnp.fl...  8.16 us
  transfers between devices with their start and end apart: 8, of which 6 were waited for; matrix products, arithmetic and copies ran while one was open for 3% of the time, Pallas kernels for 0%

profile of v1, /device:TPU:0, one launch (start us, length us, event | category | flops | bytes accessed | tf_op | source)
XLA Modules:
  0.0 325.1 jit_solution(4745151491095784361)
XLA Ops:
  6.5 0.9 convert_reduce_fusion
  7.5 1.0 fusion.56
  8.7 1.7 convolution_convert_fusion
  10.4 0.7 select_reduce_fusion.1
  11.2 9.7 %all_gather.6 = s32[4,8,8]{2,1,0:T(8,128)S(1)} all-gather(s32[1,8,8]{2,1,0:T(8,128)S(1)} %convert_element_type.87), channel_id=1, replica_groups=mesh['grp'=4,'tile'=8] {'grp'}, dimensions={0}, use_global_device_ids=true | all-gather | bytes 1280 | tf_op jit(solution)/shard_map/all_gather | solution.py:108
  20.9 0.6 copy.107
  21.5 4.9 %all-to-all-start = ((s32[4,8,8]{2,0,1:T(4,128)}), s32[4,8,8]{2,0,1:T(4,128)S(1)}, u32[]{:S(2)}, u32[]{:S(2)}) async-start(s32[4,8,8]{2,0,1:T(4,128)} %copy.107), calls=%async_computation | async-start | bytes 32768 | tf_op jit(solution)/shard_map/all_to_all | solution.py:112
  26.4 15.6 %all-gather.2.cloned.1.call-done = bf16[4,8,8,5,512]{4,2,3,1,0:T(8,128)(2,1)} async-done(((bf16[1,8,8,5,512]{4,2,3,1,0:T(8,128)(2,1)}), bf16[4,8,8,5,512]{4,2,3,1,0:T(8,128)(2,1)}) %all-gather.2.cloned.1.call-update) | async-done | bytes 1310736 | tf_op jit(solution)/shard_map/all_gather | solution.py:107
  41.9 2.5 copy.111
  44.5 4.7 %all-to-all-start.1 = ((bf16[4,8,8,5,512]{4,2,3,0,1:T(8,128)(2,1)}), bf16[4,8,8,5,512]{4,2,3,0,1:T(8,128)(2,1)S(1)}, u32[]{:S(2)}, u32[]{:S(2)}) async-start(bf16[4,8,8,5,512]{4,2,3,0,1:T(8,128)(2,1)} %copy.111), calls=%async_computation.1 | async-start | bytes 2621440 | tf_op jit(solution)/shard_map/all_to_all | solution.py:111
  49.9 2.5 copy.142
  52.4 0.7 fusion.59
  55.7 25.7 %all-to-all-done.1 = bf16[4,8,8,5,512]{4,2,3,0,1:T(8,128)(2,1)S(1)} async-done(((bf16[4,8,8,5,512]{4,2,3,0,1:T(8,128)(2,1)}), bf16[4,8,8,5,512]{4,2,3,0,1:T(8,128)(2,1)S(1)}, u32[]{:S(2)}, u32[]{:S(2)}) %all-to-all-start.1) | async-done | bytes 1310752 | tf_op jit(solution)/shard_map/all_to_all | solution.py:111
  81.6 0.6 copy.113
  82.2 2.1 broadcast_in_dim.54
  84.2 44.5 %while.14 = (s32[]{:T(128)}, f32[192,5,512]{2,1,0:T(8,128)}, s32[]{:T(128)}, s32[]{:T(128)}, s32[1024]{0:T(1024)S(1)}, /*index=5*/f32[1024,128]{1,0:T(8,128)}, f...) while((s32[]{:T(128)}, f32[192,5,512]{2,1,0:T(8,128)}, ...), condition=%wide.region_9.10_spmd.clone, body=%wide.region_6.9_spmd.clone.sunk | while | flops 178324864 | bytes 9770991 | solution.py:174
  84.3 0.6 gather_fusion
  84.9 0.8 constant_dynamic-slice_fusion.6
  85.7 4.3 %fusion.71 = f32[64,5,128]{2,1,0:T(8,128)S(1)} fusion(bf16[64,5,512]{2,1,0:T(8,128)(2,1)S(1)} %gather_fusion, s32[64,128]{1,0:T(8,128)S(1)} %constant_dynamic-slice_fusion.6), kind=kOutput, calls=%fused_computation.5.clone.1 | convolution fusion | flops 46137344 | bytes 524288 | tf_op jit(solution)/shard_map/while/body/bfc,bpc->bfp/dot_general | solution.py:152
  90.1 0.8 fusion.73
  91.0 1.0 multiply_reduce_fusion.2
  92.0 0.9 multiply_subtract_fusion.4
  92.9 1.0 multiply_subtract_fusion.5
  94.1 4.1 %fusion.75 = f32[64,15,512]{2,1,0:T(8,128)S(1)} fusion(s32[64,128]{1,0:T(8,128)S(1)} %constant_dynamic-slice_fusion.6, bf16[64,5,128]{2,1,0:T(8,128)(2,1)S(1)} %get-tuple-element.392, bf16[64,5,128]{2,1,0:T(8,128)(2,1)S(1)} %get-tuple-element.393, bf16[64,5,128]{2,1,0:T(8,128)(2,1)S(1)} %get-tuple-element.394), kind=kOutput, calls=%fused_computation.4.clone.1 | convolution fusion | flops 130760704 | bytes 2244608 | tf_op jit(solution)/shard_map/while/body/bfp,bpc->bfc/dot_general | solution.py:168
  98.4 8.1 %scatter_fusion = f32[192,5,512]{2,1,0:T(8,128)} fusion(f32[192,5,512]{2,1,0:T(8,128)} %get-tuple-element.412, s32[64]{0:T(128)S(1)} %compare_select_fusion.2, f32[64,5,512]{2,1,0:T(8,128)S(1)} %slice_add_fusion.7), kind=kCustom, calls=%fused_computation.1.clone.clone.1 | custom fusion | flops 163840 | bytes 1966336 | tf_op jit(solution)/shard_map/while/body/scatter-add | solution.py:172
  106.5 0.6 gather_fusion
  107.1 0.8 constant_dynamic-slice_fusion.6
  107.9 4.3 %fusion.71 = f32[64,5,128]{2,1,0:T(8,128)S(1)} fusion(bf16[64,5,512]{2,1,0:T(8,128)(2,1)S(1)} %gather_fusion, s32[64,128]{1,0:T(8,128)S(1)} %constant_dynamic-slice_fusion.6), kind=kOutput, calls=%fused_computation.5.clone.1 | convolution fusion | flops 46137344 | bytes 524288 | tf_op jit(solution)/shard_map/while/body/bfc,bpc->bfp/dot_general | solution.py:152
  112.3 0.8 fusion.73
  113.2 1.0 multiply_reduce_fusion.2
  114.2 0.9 multiply_subtract_fusion.4
  115.1 1.0 multiply_subtract_fusion.5
  116.3 4.1 %fusion.75 = f32[64,15,512]{2,1,0:T(8,128)S(1)} fusion(s32[64,128]{1,0:T(8,128)S(1)} %constant_dynamic-slice_fusion.6, bf16[64,5,128]{2,1,0:T(8,128)(2,1)S(1)} %get-tuple-element.392, bf16[64,5,128]{2,1,0:T(8,128)(2,1)S(1)} %get-tuple-element.393, bf16[64,5,128]{2,1,0:T(8,128)(2,1)S(1)} %get-tuple-element.394), kind=kOutput, calls=%fused_computation.4.clone.1 | convolution fusion | flops 130760704 | bytes 2244608 | tf_op jit(solution)/shard_map/while/body/bfp,bpc->bfc/dot_general | solution.py:168
  120.6 8.1 %scatter_fusion = f32[192,5,512]{2,1,0:T(8,128)} fusion(f32[192,5,512]{2,1,0:T(8,128)} %get-tuple-element.412, s32[64]{0:T(128)S(1)} %compare_select_fusion.2, f32[64,5,512]{2,1,0:T(8,128)S(1)} %slice_add_fusion.7), kind=kCustom, calls=%fused_computation.1.clone.clone.1 | custom fusion | flops 163840 | bytes 1966336 | tf_op jit(solution)/shard_map/while/body/scatter-add | solution.py:172
  128.7 3.0 copy.114
  132.0 105.4 %all_to_all.15 = f32[8,4,1,8,5,512]{5,3,1,4,2,0:T(8,128)} all-to-all(f32[8,4,1,8,5,512]{5,3,1,4,2,0:T(8,128)S(1)} %fusion.28), channel_id=1, replica_groups=mesh['grp'=4,'tile'=8] {'tile'}, dimensions={0} | all-to-all | bytes 5242880 | tf_op jit(solution)/shard_map/all_to_all | solution.py:182
  237.5 3.4 %collective-permute-start = (bf16[5,32,1,128]{3,1,2,0:T(8,128)(2,1)S(1)}, bf16[5,32,1,128]{3,1,2,0:T(8,128)(2,1)S(1)}, u32[]{:S(2)}, u32[]{:S(2)}) collective-permute-start(bf16[5,32,1,128]{3,1,2,0:T(8,128)(2,1)S(1)} %get-tuple-element.293), channel_id=1, source_target_pairs={{0,8},{8,16},{16,24},{1,9},{9,17},{17,25},{2,10},{10,18},{18,26},{... | collective-permute-start | bytes 122888 | tf_op jit(solution)/shard_map/ppermute | solution.py:14
  240.9 1.3 collective-permute-start.1
  242.2 1.0 collective-permute-done
  243.2 4.6 %collective-permute-done.1 = bf16[5,32,1,128]{3,1,2,0:T(8,128)(2,1)S(1)} collective-permute-done((bf16[5,32,1,128]{3,1,2,0:T(8,128)(2,1)S(1)}, bf16[5,32,1,128]{3,1,2,0:T(8,128)(2,1)S(1)}, u32[]{:S(2)}, u32[]{:S(2)}) %collective-permute-start.1) | collective-permute-done | bytes 40992 | tf_op jit(solution)/shard_map/ppermute | solution.py:17
  247.8 1.3 collective-permute-start.2
  249.1 1.3 collective-permute-start.3
  250.5 0.6 dynamic-slice
  251.1 1.1 collective-permute-done.3
  252.4 62.3 %all-reduce.6.cloned.1.call-done = f32[4,8,8,5,512]{4,2,0,3,1:T(8,128)} async-done(((f32[4,8,8,5,512]{4,2,0,3,1:T(8,128)}), f32[4,8,8,5,512]{4,2,0,3,1:T(8,128)}) %all-reduce.6.cloned.1.call-update) | async-done | bytes 2621456
  314.7 1.8 constant_dynamic-slice_fusion.3
  316.7 0.6 fusion.18
  317.3 0.9 copy.123
  (62 shorter events, 3.6 us)
Async XLA Ops:
  6.5 35.4 %all-gather.2.cloned.1.call-start = ((), (), s32[]{:S(2)}) async-start(), calls=%async_computation.3 | async-start | bytes 1638400 | tf_op jit(solution)/shard_map/all_gather | solution.py:107
  21.5 23.0 %all-to-all-start = ((s32[4,8,8]{2,0,1:T(4,128)}), s32[4,8,8]{2,0,1:T(4,128)S(1)}, u32[]{:S(2)}, u32[]{:S(2)}) async-start(s32[4,8,8]{2,0,1:T(4,128)} %copy.107), calls=%async_computation | async-start | bytes 32768 | tf_op jit(solution)/shard_map/all_to_all | solution.py:112
  26.4 23.5 %copy-start = (f32[1,1024,3,128]{3,1,2,0:T(8,128)S(1)}, f32[1,1024,3,128]{3,1,2,0:T(8,128)}, u32[]{:S(2)}) copy-start(f32[1,1024,3,128]{3,1,2,0:T(8,128)} %param.17) | copy-start | bytes 4718596
  44.5 10.6 %copy-start.2 = (s32[1,1024]{1,0:T(1,128)S(1)}, s32[1,1024]{1,0:T(1,128)}, u32[]{:S(2)}) copy-start(s32[1,1024]{1,0:T(1,128)} %param.16) | copy-start | bytes 12292
  44.5 36.9 %all-to-all-start.1 = ((bf16[4,8,8,5,512]{4,2,3,0,1:T(8,128)(2,1)}), bf16[4,8,8,5,512]{4,2,3,0,1:T(8,128)(2,1)S(1)}, u32[]{:S(2)}, u32[]{:S(2)}) async-start(bf16[4,8,8,5,512]{4,2,3,0,1:T(8,128)(2,1)} %copy.111), calls=%async_computation.1 | async-start | bytes 2621440 | tf_op jit(solution)/shard_map/all_to_all | solution.py:111
  49.2 265.5 %all-reduce.6.cloned.1.call-start = ((), (), s32[]{:S(2)}) async-start(), calls=%async_computation.4 | async-start | bytes 5242880
  237.4 13.0 %copy-start.1 = (f32[32,4,128]{2,1,0:T(4,128)S(1)}, f32[32,4,128]{2,1,0:T(4,128)}, u32[]{:S(2)}) copy-start(f32[32,4,128]{2,1,0:T(4,128)} %param.13) | copy-start | bytes 196612
  237.4 13.1 %copy-start.4 = (u32[32]{0:T(128)S(1)}, u32[32]{0:T(128)}, u32[]{:S(2)}) copy-start(u32[32]{0:T(128)} %constant.197) | copy-start | bytes 388
  237.5 79.3 %copy-start.3 = (s32[1,32,1]{1,2,0:T(1,128)S(1)}, s32[1,32,1]{1,2,0:T(1,128)}, u32[]{:S(2)}) copy-start(s32[1,32,1]{1,2,0:T(1,128)} %param.14) | copy-start | bytes 388
  237.5 5.8 %collective-permute-start = (bf16[5,32,1,128]{3,1,2,0:T(8,128)(2,1)S(1)}, bf16[5,32,1,128]{3,1,2,0:T(8,128)(2,1)S(1)}, u32[]{:S(2)}, u32[]{:S(2)}) collective-permute-start(bf16[5,32,1,128]{3,1,2,0:T(8,128)(2,1)S(1)} %get-tuple-element.293), channel_id=1, source_target_pairs={{0,8},{8,16},{16,24},{1,9},{9,17},{17,25},{2,10},{10,18},{18,26},{... | collective-permute-start | bytes 122888 | tf_op jit(solution)/shard_map/ppermute | solution.py:14
  240.9 6.9 %collective-permute-start.1 = (bf16[5,32,1,128]{3,1,2,0:T(8,128)(2,1)S(1)}, bf16[5,32,1,128]{3,1,2,0:T(8,128)(2,1)S(1)}, u32[]{:S(2)}, u32[]{:S(2)}) collective-permute-start(bf16[5,32,1,128]{3,1,2,0:T(8,128)(2,1)S(1)} %get-tuple-element.294), channel_id=1, source_target_pairs={{8,0},{16,8},{24,16},{9,1},{17,9},{25,17},{10,2},{18,10},{26,18},{... | collective-permute-start | bytes 122888 | tf_op jit(solution)/shard_map/ppermute | solution.py:17
  247.8 3.3 %collective-permute-start.2 = (bf16[5,1,6,128]{3,1,2,0:T(2,128)(2,1)S(1)}, bf16[5,1,6,128]{3,1,2,0:T(2,128)(2,1)S(1)}, u32[]{:S(2)}, u32[]{:S(2)}) collective-permute-start(bf16[5,1,6,128]{3,1,2,0:T(2,128)(2,1)S(1)} %get-tuple-element.291), channel_id=1, source_target_pairs={{0,1},{1,2},{2,3},{3,4},{4,5},{5,6},{6,7},{8,9},{9,10},{10,11},{11... | collective-permute-start | bytes 23048 | tf_op jit(solution)/shard_map/ppermute | solution.py:14
  249.1 3.1 collective-permute-start.3
Sparse Core Ops, SparseCore 0:
  10.5 31.3 all-gather.1
  237.6 77.0 all-reduce.5
